TPU v7x, 32 devices: a whole 2x2x4 slice. The times are simulated.
32 devices in a mesh: groups: 2 (over y), expert: 4 (over z), dp: 2 (over x), inner: 2 (over core).
Axes of the slice: x: 2, y: 2, z: 4, core: 2. Of those that a mesh axis runs over, the one named last changes fastest.
Arguments:
- tokens: bfloat16 [2048, 2048], P(('groups', 'expert', 'inner'), 'dp'), parts along dimension 0, may hold values from -6 to 6
- out_grad: bfloat16 [2048, 2048], P(('groups', 'expert', 'inner'), 'dp'), parts along dimension 0, may hold values from -2.5 to 2.5
- expert_ids: int32 [2048, 2], P(('groups', 'expert', 'inner')), parts along dimension 0, may hold values from 0 to 7, all different within a row; in each aligned block of 128 rows (0 to 127, 128 to 255, ...) at most 48 rows name the same one
- gate_weights: float32 [2048, 2], P(('groups', 'expert', 'inner')), parts along dimension 0, may hold values from 0.2 to 1
- shadow_expert: int32 [4], replicated, may hold values from 0 to 7, as said below
- w_gate: bfloat16 [8, 2048, 1024], P('expert', 'dp', 'inner'), may hold values from -0.125 to 0.125
- w_up: bfloat16 [8, 2048, 1024], P('expert', 'dp', 'inner'), may hold values from -0.125 to 0.125
- w_down: bfloat16 [8, 1024, 2048], P('expert', 'inner', 'dp'), may hold values from -0.1875 to 0.1875
- copy_gate: bfloat16 [4, 2048, 1024], P('expert', 'dp', 'inner'), may hold values from -0.125 to 0.125
- copy_up: bfloat16 [4, 2048, 1024], P('expert', 'dp', 'inner'), may hold values from -0.125 to 0.125
- copy_down: bfloat16 [4, 1024, 2048], P('expert', 'inner', 'dp'), may hold values from -0.1875 to 0.1875
Outputs:
- grad_tokens: bfloat16 [2048, 2048], P(('groups', 'expert', 'inner'), 'dp'), parts along dimension 0
- grad_w_gate: bfloat16 [16, 2048, 1024], P(('groups', 'expert'), 'dp', 'inner'), parts along dimension 0
- grad_w_up: bfloat16 [16, 2048, 1024], P(('groups', 'expert'), 'dp', 'inner'), parts along dimension 0
- grad_w_down: bfloat16 [16, 1024, 2048], P(('groups', 'expert'), 'inner', 'dp'), parts along dimension 0
There are 2 independent parts, one for each index of `groups`. A program takes and returns all parts, laid end to end along the dimension named above; an argument that names none is the same for every part. Nothing has to cross between parts.
Inputs may be any that keep to these rules, and one draw needn't show every extreme that they name: `expert_ids`: A token's two experts differ; among the 128 tokens of one index of expert+inner no expert is named more than 48 times, a bound that some block reaches. Experts 2 j and 2 j + 1 are owned by index j of expert. `shadow_expert`: entry j names an expert that index j does not own. Exactly half of the indices of expert own the experts of two entries each, the other indices those of none; the two entries that fall on one index may name the same expert or its two experts.
All inputs are finite; a program needn't handle non-finite values.
Results may differ from a plain program's by a relative error of at most 0.02.
Values may be sent and summed in bfloat16 or wider, within the bound.
A program may use at most 128 MiB of HBM per device.

v0:
```python
import jax
import jax.numpy as jnp
from jax import lax
from jax.sharding import PartitionSpec as P


def serving_copy(expert_ids, shadow_expert, first_token):
    tok_rows = expert_ids.shape[0]
    shadow_count = shadow_expert.shape[0]
    token_index = first_token + jnp.arange(tok_rows, dtype=jnp.int32)
    position = token_index[:, None] + jnp.arange(2, dtype=jnp.int32)[None, :]
    matches = (expert_ids[:, :, None] == shadow_expert[None, None, :]).astype(jnp.int32)
    copies = 1 + jnp.sum(matches, axis=2)
    chosen = position % copies
    slot_order = jnp.arange(shadow_count, dtype=jnp.int32)
    lower_slot = (slot_order[:, None] > slot_order[None, :]).astype(jnp.int32)
    same_expert = (shadow_expert[:, None] == shadow_expert[None, :]).astype(jnp.int32)
    rank_among = jnp.sum(lower_slot * same_expert, axis=1)
    picked = matches * (rank_among[None, None, :] == chosen[:, :, None] - 1).astype(jnp.int32)
    holder = jnp.sum(picked * slot_order[None, None, :], axis=2)
    shadowed = jnp.sum(picked, axis=2)
    return jnp.where(shadowed > 0, 2 * shadow_count + holder, expert_ids)


def activation(block_sums):
    width_half = block_sums.shape[-1] // 3
    pre_gate = block_sums[..., :width_half]
    pre_up = block_sums[..., width_half : 2 * width_half]
    hidden_grad = block_sums[..., 2 * width_half :]
    sigmoid_gate = jax.nn.sigmoid(pre_gate)
    swish_gate = pre_gate * sigmoid_gate
    grad_up = (hidden_grad * swish_gate).astype(jnp.bfloat16)
    grad_gate = (
        hidden_grad * pre_up * sigmoid_gate * (1.0 + pre_gate * (1.0 - sigmoid_gate))
    ).astype(jnp.bfloat16)
    hidden = (swish_gate * pre_up).astype(jnp.bfloat16)
    return (grad_gate, grad_up, hidden)


def on_device(
    tokens,
    out_grad,
    expert_ids,
    gate_weights,
    shadow_expert,
    w_gate,
    w_up,
    w_down,
    copy_gate,
    copy_up,
    copy_down,
):
    tok_rows, feature_piece = tokens.shape
    hidden_piece = w_gate.shape[2]
    expert_count = lax.axis_size("expert")
    inner_count = lax.axis_size("inner")
    capacity = max(2, 3 * tok_rows // (2 * expert_count))
    owned_total = 2 * expert_count
    block_number = lax.axis_index("expert") * inner_count + lax.axis_index("inner")
    copy_ids = serving_copy(expert_ids, shadow_expert, block_number * tok_rows)
    flat_ids = copy_ids.reshape(-1)
    holder_index = jnp.where(flat_ids < owned_total, flat_ids // 2, flat_ids - owned_total)
    slot_kind = jnp.where(flat_ids < owned_total, flat_ids % 2, 2)
    copy_onehot = (
        flat_ids[:, None] == jnp.arange(3 * expert_count, dtype=jnp.int32)[None, :]
    ).astype(jnp.int32)
    route_rank = jnp.sum((jnp.cumsum(copy_onehot, axis=0) - 1) * copy_onehot, axis=1)
    slot_place = ((slot_kind * expert_count + holder_index) * capacity + route_rank).reshape(
        tok_rows, 2
    )
    send_slots = 3 * expert_count * capacity
    slot_range = jnp.arange(send_slots, dtype=jnp.int32)
    route_hit = (slot_range[:, None, None] == slot_place[None, :, :]).astype(jnp.float32)
    place_matrix = jnp.sum(route_hit, axis=2)
    gate_matrix = jnp.sum(route_hit * gate_weights[None, :, :], axis=2)
    rows_in = jnp.dot(
        place_matrix.astype(jnp.bfloat16), tokens, preferred_element_type=jnp.float32
    ).astype(jnp.bfloat16)
    rows_grad = jnp.dot(
        gate_matrix, out_grad.astype(jnp.float32), precision=lax.Precision.HIGHEST
    ).astype(jnp.bfloat16)

    def duplicate(values):
        shaped = values.reshape(3, expert_count, 1, capacity, feature_piece)
        widened = jnp.broadcast_to(shaped, (3, expert_count, inner_count, capacity, feature_piece))
        return widened.reshape(3, expert_count * inner_count, capacity, feature_piece)

    recv_in, recv_grad = (
        lax.all_to_all(
            duplicate(rows_in), ("expert", "inner"), split_axis=1, concat_axis=1, tiled=True
        ),
        lax.all_to_all(
            duplicate(rows_grad), ("expert", "inner"), split_axis=1, concat_axis=1, tiled=True
        ),
    )
    host_rows = expert_count * inner_count * capacity
    inputs = recv_in.reshape(3, host_rows, feature_piece)
    grad_rows = recv_grad.reshape(3, host_rows, feature_piece)
    weight_gate = jnp.concatenate([w_gate, copy_gate], axis=0)
    weight_up = jnp.concatenate([w_up, copy_up], axis=0)
    weight_down = jnp.concatenate([w_down, copy_down], axis=0)
    partial_sums = jnp.concatenate(
        [
            jnp.einsum("srf,sfh->srh", inputs, weight_gate, preferred_element_type=jnp.float32),
            jnp.einsum("srf,sfh->srh", inputs, weight_up, preferred_element_type=jnp.float32),
            jnp.einsum("srf,shf->srh", grad_rows, weight_down, preferred_element_type=jnp.float32),
        ],
        axis=2,
    )
    block_sums = lax.psum(partial_sums.astype(jnp.bfloat16), "dp").astype(jnp.float32)
    grad_gate, grad_up, hidden = activation(block_sums)
    route_part = jnp.einsum(
        "srh,sfh->srf", grad_gate, weight_gate, preferred_element_type=jnp.float32
    )
    route_part = route_part + jnp.einsum(
        "srh,sfh->srf", grad_up, weight_up, preferred_element_type=jnp.float32
    )
    returned = lax.all_to_all(
        route_part.reshape(3, expert_count * inner_count, capacity, feature_piece).astype(
            jnp.bfloat16
        ),
        ("expert", "inner"),
        split_axis=1,
        concat_axis=1,
        tiled=True,
    ).astype(jnp.float32)
    returned = jnp.sum(
        returned.reshape(3, expert_count, inner_count, capacity, feature_piece), axis=2
    ).reshape(send_slots, feature_piece)
    grad_tokens = jnp.dot(place_matrix.T, returned, precision=lax.Precision.HIGHEST).astype(
        jnp.bfloat16
    )
    dw_gate = jnp.einsum("srf,srh->sfh", inputs, grad_gate, preferred_element_type=jnp.float32)
    dw_up = jnp.einsum("srf,srh->sfh", inputs, grad_up, preferred_element_type=jnp.float32)
    dw_down = jnp.einsum("srh,srf->shf", hidden, grad_rows, preferred_element_type=jnp.float32)
    shadow_panel = jnp.concatenate(
        [
            dw_gate[2].astype(jnp.bfloat16).reshape(expert_count, -1),
            dw_up[2].astype(jnp.bfloat16).reshape(expert_count, -1),
            dw_down[2].astype(jnp.bfloat16).reshape(expert_count, -1),
        ],
        axis=1,
    )
    spread_pieces = lax.all_to_all(shadow_panel, "expert", split_axis=0, concat_axis=0, tiled=True)
    piece_width = spread_pieces.shape[1]
    indicator = (
        shadow_expert[:, None] == jnp.arange(owned_total, dtype=jnp.int32)[None, :]
    ).astype(jnp.float32)
    per_expert = jnp.dot(
        indicator.T, spread_pieces.astype(jnp.float32), precision=lax.Precision.HIGHEST
    )
    collected = lax.all_to_all(
        per_expert.reshape(expert_count, 2, piece_width).astype(jnp.bfloat16),
        "expert",
        split_axis=0,
        concat_axis=0,
        tiled=True,
    ).astype(jnp.float32)
    collected = jnp.transpose(collected, (1, 0, 2))
    third = piece_width // 3
    gate_extra = collected[:, :, :third].reshape(2, feature_piece, hidden_piece)
    up_extra = collected[:, :, third : 2 * third].reshape(2, feature_piece, hidden_piece)
    down_extra = collected[:, :, 2 * third :].reshape(2, hidden_piece, feature_piece)
    grad_w_gate = (dw_gate[:2] + gate_extra).astype(jnp.bfloat16)
    grad_w_up = (dw_up[:2] + up_extra).astype(jnp.bfloat16)
    grad_w_down = (dw_down[:2] + down_extra).astype(jnp.bfloat16)
    return (grad_tokens, grad_w_gate, grad_w_up, grad_w_down)


def solution(mesh):
    return jax.shard_map(
        on_device,
        mesh=mesh,
        in_specs=(
            P(("groups", "expert", "inner"), "dp"),
            P(("groups", "expert", "inner"), "dp"),
            P(("groups", "expert", "inner"), None),
            P(("groups", "expert", "inner"), None),
            P(),
            P("expert", "dp", "inner"),
            P("expert", "dp", "inner"),
            P("expert", "inner", "dp"),
            P("expert", "dp", "inner"),
            P("expert", "dp", "inner"),
            P("expert", "inner", "dp"),
        ),
        out_specs=(
            P(("groups", "expert", "inner"), "dp"),
            P(("groups", "expert"), "dp", "inner"),
            P(("groups", "expert"), "dp", "inner"),
            P(("groups", "expert"), "inner", "dp"),
        ),
        check_vma=False,
    )
```

profile of v0, /device:TPU:0, one launch (start us, length us, event | category | flops | bytes accessed | tf_op | source)
XLA Modules:
  0.0 639.0 jit_solution(14092023790676570305)
XLA Ops:
  15.4 6.5 %all-to-all-start = ((bf16[3,8,48,1024]{3,2,0,1:T(8,128)(2,1)}), bf16[3,8,48,1024]{3,2,0,1:T(8,128)(2,1)S(1)}, u32[]{:S(2)}, u32[]{:S(2)}) async-start(bf16[3,8,48,1024]{3,2,0,1:T(8,128)(2,1)} %bitcast.49), calls=%async_computation | async-start | bytes 4718592 | tf_op jit(solution)/shard_map/all_to_all | solution.py:89
  24.2 52.4 %all-to-all-done = bf16[3,8,48,1024]{3,2,0,1:T(8,128)(2,1)S(1)} async-done(((bf16[3,8,48,1024]{3,2,0,1:T(8,128)(2,1)}), bf16[3,8,48,1024]{3,2,0,1:T(8,128)(2,1)S(1)}, u32[]{:S(2)}, u32[]{:S(2)}) %all-to-all-start) | async-done | bytes 2359328 | tf_op jit(solution)/shard_map/all_to_all | solution.py:89
  95.6 43.8 %all-to-all-done.1 = bf16[3,8,48,1024]{3,2,0,1:T(8,128)(2,1)} async-done(((bf16[3,8,48,1024]{3,2,0,1:T(8,128)(2,1)}), bf16[3,8,48,1024]{3,2,0,1:T(8,128)(2,1)}, u32[]{:S(2)}, u32[]{:S(2)}) %all-to-all-start.1) | async-done | bytes 2359328 | tf_op jit(solution)/shard_map/all_to_all | solution.py:92
  146.2 93.5 %all-reduce.2.cloned.1.call-done = bf16[3,384,1536]{2,1,0:T(8,128)(2,1)} async-done(((bf16[3,384,1536]{2,1,0:T(8,128)(2,1)}), bf16[3,384,1536]{2,1,0:T(8,128)(2,1)}) %all-reduce.2.cloned.1.call-update) | async-done | bytes 3538960 | tf_op jit(solution)/shard_map/psum | solution.py:110
  271.6 8.8 %maximum_bitcast_fusion = bf16[4,1,393216]{2,0,1:T(4,128)(2,1)S(1)} fusion(bf16[4,131072]{1,0:T(4,128)(2,1)} %convert_element_type.95, bf16[4,131072]{1,0:T(4,128)(2,1)} %convert_element_type.93, bf16[4,131072]{1,0:T(4,128)(2,1)} %convert_element_type.92), kind=kLoop, calls=%fused_computation.15 | loop fusion | flops 9437184 | bytes 6291456 | tf_op jit(solution)/shard_map/all_to_all | solution.py:144
  280.9 6.3 reduce.2
  287.2 6.8 %reshape.192 = bf16[4,2,196608]{2,1,0:T(2,128)(2,1)} reshape(bf16[4,393216]{1,0:T(4,128)(2,1)} %reduce.2) | data formatting | bytes 6291456
  294.0 4.8 all-to-all-start.3
  305.3 64.3 %all-to-all-done.3 = bf16[4,2,196608]{2,1,0:T(2,128)(2,1)} async-done(((bf16[4,2,196608]{2,1,0:T(2,128)(2,1)}), bf16[4,2,196608]{2,1,0:T(2,128)(2,1)}, u32[]{:S(2)}, u32[]{:S(2)}) %all-to-all-start.3) | async-done | bytes 3145760 | tf_op jit(solution)/shard_map/all_to_all | solution.py:144
  369.6 4.8 all-to-all-start.2
  374.5 6.2 reshape.193
  380.6 7.9 %convolution_convert_fusion = bf16[4,2,393216]{2,0,1:T(4,128)(2,1)S(1)} fusion(bf16[4,1,393216]{2,1,0:T(2,128)(2,1)} %reshape.193, s32[4,2]{0,1:T(2,128)S(1)} %multiply_add_fusion, s32[4]{0:T(128)S(1)} %copy-done.24), kind=kOutput, calls=%fused_computation | convolution fusion | flops 28311584 | bytes 9437232 | tf_op jit(solution)/shard_map/dot_general | solution.py:149
  388.6 20.6 %copy.111 = bf16[4,2,393216]{2,1,0:T(2,128)(2,1)} copy(bf16[4,2,393216]{2,0,1:T(4,128)(2,1)S(1)} %convolution_convert_fusion) | data formatting | bytes 12582912 | tf_op jit(solution)/shard_map/convert_element_type | solution.py:153
  409.1 20.0 %all-to-all-done.2 = bf16[3,8,48,1024]{3,2,0,1:T(8,128)(2,1)} async-done(((bf16[3,8,48,1024]{3,2,0,1:T(8,128)(2,1)}), bf16[3,8,48,1024]{3,2,0,1:T(8,128)(2,1)}, u32[]{:S(2)}, u32[]{:S(2)}) %all-to-all-start.2) | async-done | bytes 2359328 | tf_op jit(solution)/shard_map/all_to_all | solution.py:118
  429.1 5.5 all-to-all-start.4
  440.5 132.3 %all-to-all-done.4 = bf16[4,2,393216]{2,1,0:T(2,128)(2,1)} async-done(((bf16[4,2,393216]{2,1,0:T(2,128)(2,1)}), bf16[4,2,393216]{2,1,0:T(2,128)(2,1)}, u32[]{:S(2)}, u32[]{:S(2)}) %all-to-all-start.4) | async-done | bytes 6291488 | tf_op jit(solution)/shard_map/all_to_all | solution.py:152
  572.7 6.7 %convert_bitcast_fusion = f32[2,4,393216]{2,0,1:T(2,128)S(1)} fusion(bf16[4,2,393216]{2,1,0:T(2,128)(2,1)} %all-to-all-done.4), kind=kLoop, calls=%fused_computation.1 | loop fusion | flops 3145728 | bytes 18874368 | tf_op jit(solution)/shard_map/transpose | solution.py:159
  587.9 5.8 reshape.186
  593.7 5.7 fusion
  604.1 6.0 reshape.185
  610.1 5.7 fusion.1
  615.8 4.8 copy.112
  620.5 5.8 reshape.184
  626.4 5.5 fusion.2
  (118 shorter events, 94.0 us)
Async XLA Ops:
  7.2 5.8 copy-start
  15.4 6.5 %copy-start.23 = (bf16[128,1024]{1,0:T(8,128)(2,1)S(1)}, bf16[128,1024]{1,0:T(8,128)(2,1)}, u32[]{:S(2)}) copy-start(bf16[128,1024]{1,0:T(8,128)(2,1)} %param.12) | copy-start | bytes 786436
  15.4 61.1 %all-to-all-start = ((bf16[3,8,48,1024]{3,2,0,1:T(8,128)(2,1)}), bf16[3,8,48,1024]{3,2,0,1:T(8,128)(2,1)S(1)}, u32[]{:S(2)}, u32[]{:S(2)}) async-start(bf16[3,8,48,1024]{3,2,0,1:T(8,128)(2,1)} %bitcast.49), calls=%async_computation | async-start | bytes 4718592 | tf_op jit(solution)/shard_map/all_to_all | solution.py:89
  76.6 3.9 copy-start.9
  80.4 59.0 %all-to-all-start.1 = ((bf16[3,8,48,1024]{3,2,0,1:T(8,128)(2,1)}), bf16[3,8,48,1024]{3,2,0,1:T(8,128)(2,1)}, u32[]{:S(2)}, u32[]{:S(2)}) async-start(bf16[3,8,48,1024]{3,2,0,1:T(8,128)(2,1)} %bitcast.48), calls=%async_computation.1 | async-start | bytes 4718592 | tf_op jit(solution)/shard_map/all_to_all | solution.py:92
  84.8 154.8 %all-reduce.2.cloned.1.call-start = ((), (), s32[]{:S(2)}) async-start(), calls=%async_computation.5 | async-start | bytes 7077888 | tf_op jit(solution)/shard_map/psum | solution.py:110
  87.4 3.4 copy-start.8
  87.4 3.1 copy-start.10
  90.5 2.7 copy-start.11
  139.5 2.6 copy-start.26
  242.6 2.8 copy-start.17
  247.4 2.6 copy-start.13
  257.2 2.6 copy-start.3
  267.0 2.6 copy-start.2
  294.0 4.8 copy-start.6
  294.0 75.7 %all-to-all-start.3 = ((bf16[4,2,196608]{2,1,0:T(2,128)(2,1)}), bf16[4,2,196608]{2,1,0:T(2,128)(2,1)}, u32[]{:S(2)}, u32[]{:S(2)}) async-start(bf16[4,2,196608]{2,1,0:T(2,128)(2,1)} %reshape.192), calls=%async_computation.3 | async-start | bytes 6291456 | tf_op jit(solution)/shard_map/all_to_all | solution.py:144
  298.8 3.5 copy-start.7
  298.8 3.5 copy-start.12
  369.6 59.5 %all-to-all-start.2 = ((bf16[3,8,48,1024]{3,2,0,1:T(8,128)(2,1)}), bf16[3,8,48,1024]{3,2,0,1:T(8,128)(2,1)}, u32[]{:S(2)}, u32[]{:S(2)}) async-start(bf16[3,8,48,1024]{3,2,0,1:T(8,128)(2,1)} %copy.105), calls=%async_computation.2 | async-start | bytes 4718592 | tf_op jit(solution)/shard_map/all_to_all | solution.py:118
  374.5 6.2 copy-start.24
  429.1 143.6 %all-to-all-start.4 = ((bf16[4,2,393216]{2,1,0:T(2,128)(2,1)}), bf16[4,2,393216]{2,1,0:T(2,128)(2,1)}, u32[]{:S(2)}, u32[]{:S(2)}) async-start(bf16[4,2,393216]{2,1,0:T(2,128)(2,1)} %copy.111), calls=%async_computation.4 | async-start | bytes 12582912 | tf_op jit(solution)/shard_map/all_to_all | solution.py:152
  593.7 5.7 copy-start.5
  610.1 5.7 copy-start.4
  626.4 5.5 copy-start.1
  (9 other events, 16.0 us)
Sparse Core Ops, SparseCore 0:
  146.3 93.2 all-reduce.1
where the time goes:
time: 646 us; the launch traced here: 639 us
  waiting for transfers between devices  406 us (63%)
  local copies, waits for them, and re-layouts  107 us (17%)
  other arithmetic  53.9 us (8%)
  matrix products  31.1 us (5%)
  starting transfers between devices  26 us (4%)
  between operations  14.7 us (2%)
    all_to_all x1, waiting for transfers between devices, on_device(): lax.all_to_all(per_expert.reshape(expert_count, 2, piece_width).astype(jn...  132 us
    psum x1, waiting for transfers between devices, on_device(): lax.psum(partial_sums.astype(jnp.bfloat16), 'dp').astype(jnp.float32)  93.5 us
    all_to_all x1, waiting for transfers between devices, on_device(): lax.all_to_all(shadow_panel, 'expert', split_axis=0, concat_axis=0, tiled...  64.3 us
    all_to_all x1, waiting for transfers between devices, on_device(): lax.all_to_all(duplicate(rows_in), ('expert', 'inner'), split_axis=1, con...  52.4 us
    all_to_all x1, waiting for transfers between devices, on_device(): lax.all_to_all(duplicate(rows_grad), ('expert', 'inner'), split_axis=1, c...  43.8 us
    unnamed x60, local copies, waits for them, and re-layouts  28.3 us
    convert_element_type x1, local copies, waits for them, and re-layouts, on_device(): per_expert.reshape(expert_count, 2, piece_width).astype(jnp.bfloat16)  20.6 us
    all_to_all x1, waiting for transfers between devices, on_device(): lax.all_to_all(route_part.reshape(3, expert_count * inner_count, capacity...  20 us
  transfers between devices with their start and end apart: 6, of which 6 were waited for; matrix products, arithmetic and copies ran while one was open for 9% of the time, Pallas kernels for 0%

commit v1 on v0

v1 whole, which is shorter than its diff:
```python
import jax
import jax.numpy as jnp
from jax import lax
from jax.sharding import PartitionSpec as P

BF16 = jnp.bfloat16
F32 = jnp.float32


def serving_copy(ids, shadow_expert, token_index):
    shadow_count = shadow_expert.shape[0]
    position = token_index[None, :] + jnp.arange(2, dtype=jnp.int32)[:, None]
    matches = (ids[None] == shadow_expert[:, None, None]).astype(jnp.int32)
    copies = 1 + jnp.sum(matches, axis=0)
    chosen = position % copies
    slot_order = jnp.arange(shadow_count, dtype=jnp.int32)
    lower_slot = (slot_order[:, None] > slot_order[None, :]).astype(jnp.int32)
    same_expert = (shadow_expert[:, None] == shadow_expert[None, :]).astype(jnp.int32)
    rank_among = jnp.sum(lower_slot * same_expert, axis=1)
    picked = matches * (rank_among[:, None, None] == chosen[None] - 1).astype(jnp.int32)
    holder = jnp.sum(picked * slot_order[:, None, None], axis=0)
    shadowed = jnp.sum(picked, axis=0)
    return jnp.where(shadowed > 0, 2 * shadow_count + holder, ids)


def activation(pre_gate, pre_up, hidden_grad, served):
    sig = jax.nn.sigmoid(pre_gate)
    swish = pre_gate * sig
    grad_up = hidden_grad * swish
    grad_gate = hidden_grad * pre_up * sig * (1.0 + pre_gate * (1.0 - sig))
    hidden = swish * pre_up
    keep = served[:, None] > 0
    wide = jnp.concatenate([grad_gate, grad_up, hidden], axis=1)
    return jnp.where(keep, wide, 0.0).astype(BF16)


def mm(a, b, ca, cb):
    return lax.dot_general(a, b, (((ca,), (cb,)), ((), ())), preferred_element_type=F32)


def on_device(
    tokens,
    out_grad,
    expert_ids,
    gate_weights,
    shadow_expert,
    w_gate,
    w_up,
    w_down,
    copy_gate,
    copy_up,
    copy_down,
):
    tok_rows, features = tokens.shape
    width = w_gate.shape[2]
    expert_count = lax.axis_size("expert")
    inner_count = lax.axis_size("inner")
    dp_count = lax.axis_size("dp")
    blocks = expert_count * inner_count
    total = blocks * tok_rows
    capacity = max(2, 3 * tok_rows // (2 * expert_count))
    rows = blocks * capacity
    me = lax.axis_index("expert")
    both = ("expert", "inner")

    meta = jnp.concatenate([expert_ids.astype(F32).T, gate_weights.T], axis=0)
    meta = lax.all_gather(meta, both, axis=0, tiled=False)
    meta = jnp.transpose(meta, (1, 0, 2)).reshape(4, total)
    tokens_all = lax.all_gather(tokens, both, axis=0, tiled=True)
    grads_all = lax.all_gather(out_grad, both, axis=0, tiled=True)

    ids = meta[:2].astype(jnp.int32)
    gates = meta[2:]
    copy_ids = serving_copy(ids, shadow_expert, jnp.arange(total, dtype=jnp.int32))
    slot_expert = jnp.stack([2 * me, 2 * me + 1, shadow_expert[me]])
    slot_copy = jnp.stack([2 * me, 2 * me + 1, 2 * expert_count + me])
    member = ids[None] == slot_expert[:, None, None]
    named = jnp.sum(member.astype(F32), axis=1)
    gate_of = jnp.sum(jnp.where(member, gates[None], 0.0), axis=1)
    served_of = jnp.sum((copy_ids[None] == slot_copy[:, None, None]).astype(F32), axis=1)
    before = (jnp.arange(tok_rows)[:, None] < jnp.arange(tok_rows)[None, :]).astype(BF16)
    rank = jnp.dot(
        named.reshape(3 * blocks, tok_rows).astype(BF16), before, preferred_element_type=F32
    ).astype(jnp.int32)
    rank = rank.reshape(3, blocks, tok_rows)
    place = rank + capacity * jnp.arange(blocks, dtype=jnp.int32)[None, :, None]
    place = jnp.where(named > 0, place.reshape(3, total), -1)
    hit = place[:, None, :] == jnp.arange(rows, dtype=jnp.int32)[None, :, None]
    gate_row = jnp.sum(jnp.where(hit, gate_of[:, None, :], 0.0), axis=2)
    served_row = jnp.sum(jnp.where(hit, served_of[:, None, :], 0.0), axis=2)
    select = hit.astype(BF16)
    select_all = select.reshape(3 * rows, total)

    inputs = mm(select_all, tokens_all, 1, 0).astype(BF16).reshape(3, rows, features)
    scaled = (mm(select_all, grads_all, 1, 0) * gate_row.reshape(-1, 1)).astype(BF16)
    scaled = scaled.reshape(3, rows, features)

    gate_w = (w_gate[0], w_gate[1], copy_gate[0])
    up_w = (w_up[0], w_up[1], copy_up[0])
    down_w = (w_down[0], w_down[1], copy_down[0])

    def settle(values):
        if dp_count == 2:
            other = lax.ppermute(values, "dp", [(0, 1), (1, 0)])
            return values.astype(F32) + other.astype(F32)
        return lax.psum(values, "dp").astype(F32)

    def acts_of(s):
        part = jnp.concatenate(
            [
                mm(inputs[s], gate_w[s], 1, 0).astype(BF16),
                mm(inputs[s], up_w[s], 1, 0).astype(BF16),
                mm(scaled[s], down_w[s], 1, 1).astype(BF16),
            ],
            axis=1,
        )
        sums = settle(part)
        return activation(
            sums[:, :width], sums[:, width : 2 * width], sums[:, 2 * width :], served_row[s]
        )

    acts = [None, None, acts_of(2)]
    shadow_acts = lax.all_gather(acts[2], "expert", axis=0, tiled=False)
    acts[0] = acts_of(0)
    acts[1] = acts_of(1)

    route = [
        (
            mm(acts[s][:, :width], gate_w[s], 1, 1)
            + mm(acts[s][:, width : 2 * width], up_w[s], 1, 1)
        ).astype(BF16)
        for s in range(3)
    ]
    route_all = jnp.concatenate(route, axis=0)
    token_part = mm(select_all, route_all, 0, 0).astype(BF16)
    grad_tokens = lax.psum_scatter(token_part, both, scatter_dimension=0, tiled=True)

    out_gate, out_up, out_down = [], [], []
    for s in range(2):
        takes = (shadow_expert == slot_expert[s]).astype(F32)
        whole = acts[s].astype(F32)
        for j in range(expert_count):
            whole = whole + jnp.where(takes[j] > 0, shadow_acts[j].astype(F32), 0.0)
        whole = whole.astype(BF16)
        out_gate.append(mm(inputs[s], whole[:, :width], 0, 0).astype(BF16))
        out_up.append(mm(inputs[s], whole[:, width : 2 * width], 0, 0).astype(BF16))
        out_down.append(mm(whole[:, 2 * width :], scaled[s], 0, 0).astype(BF16))
    return (grad_tokens, jnp.stack(out_gate), jnp.stack(out_up), jnp.stack(out_down))


def solution(mesh):
    return jax.shard_map(
        on_device,
        mesh=mesh,
        in_specs=(
            P(("groups", "expert", "inner"), "dp"),
            P(("groups", "expert", "inner"), "dp"),
            P(("groups", "expert", "inner"), None),
            P(("groups", "expert", "inner"), None),
            P(),
            P("expert", "dp", "inner"),
            P("expert", "dp", "inner"),
            P("expert", "inner", "dp"),
            P("expert", "dp", "inner"),
            P("expert", "dp", "inner"),
            P("expert", "inner", "dp"),
        ),
        out_specs=(
            P(("groups", "expert", "inner"), "dp"),
            P(("groups", "expert"), "dp", "inner"),
            P(("groups", "expert"), "dp", "inner"),
            P(("groups", "expert"), "inner", "dp"),
        ),
        check_vma=False,
    )
```

time: 646 us -> 254 us (0.39)
  waiting for transfers between devices: 406 us -> 150 us
  local copies, waits for them, and re-layouts: 107 us -> 8.48 us
  other arithmetic: 53.9 us -> 23.9 us
  starting transfers between devices: 26 us -> 4.26 us
  blocking collectives: 0 us -> 14.5 us
    all_to_all x5 -> x0, waiting for transfers between devices: 313 us -> none  [the longest x1 132 us: on_device(): lax.all_to_all(per_expert.reshape(expert_count, 2, piece_width).astype(jn...]
    psum x1 -> x0, waiting for transfers between devices: 93.5 us -> none  [on_device(): lax.psum(partial_sums.astype(jnp.bfloat16), 'dp').astype(jnp.float32)]
    ppermute x0 -> x3, waiting for transfers between devices: none -> 66.1 us  [settle(): other = lax.ppermute(values, 'dp', [(0, 1), (1, 0)])]
    all_gather x0 -> x3, waiting for transfers between devices: none -> 60.3 us  [the longest x1 27.3 us: on_device(): shadow_acts = lax.all_gather(acts[2], 'expert', axis=0, tiled=False)]
    convert_element_type x5 -> x1, local copies, waits for them, and re-layouts: 29.9 us -> 0.02 us  [on_device(): named.reshape(3 * blocks, tok_rows).astype(BF16)]
    all_to_all x5 -> x0, starting transfers between devices: 26 us -> none  [the longest x1 6.49 us: on_device(): lax.all_to_all(duplicate(rows_in), ('expert', 'inner'), split_axis=1, con...]
    reduce_scatter x0 -> x1, waiting for transfers between devices: none -> 22.1 us  [on_device(): lax.psum_scatter(token_part, both, scatter_dimension=0, tiled=True)]
    unnamed x60 -> x52, local copies, waits for them, and re-layouts: 28.3 us -> 6.43 us
  transfers between devices with their start and end apart: 6 -> 7, of which waited for: 6 -> 7; matrix products, arithmetic and copies ran while one was open for 9% -> 15% of each run, Pallas kernels for 0% -> 0%
where the time goes in v1:
time: 254 us; the launch traced here: 253 us
  waiting for transfers between devices  150 us (59%)
  matrix products  32.8 us (13%)
  other arithmetic  23.9 us (9%)
  between operations  19.2 us (8%)
  blocking collectives  14.5 us (6%)
  local copies, waits for them, and re-layouts  8.48 us (3%)
  starting transfers between devices  4.26 us (2%)
    ppermute x3, waiting for transfers between devices, settle(): other = lax.ppermute(values, 'dp', [(0, 1), (1, 0)])  66.1 us
    dot_general x24, matrix products, mm(): lax.dot_general(a, b, (((ca,), (cb,)), ((), ())), preferred_element_type=...  32.7 us
    all_gather x1, waiting for transfers between devices, on_device(): shadow_acts = lax.all_gather(acts[2], 'expert', axis=0, tiled=False)  27.3 us
    all_gather x1, waiting for transfers between devices, on_device(): grads_all = lax.all_gather(out_grad, both, axis=0, tiled=True)  23.7 us
    reduce_scatter x1, waiting for transfers between devices, on_device(): lax.psum_scatter(token_part, both, scatter_dimension=0, tiled=True)  22.1 us
    all_gather x1, blocking collectives, on_device(): meta = lax.all_gather(meta, both, axis=0, tiled=False)  14.5 us
    all_gather x1, waiting for transfers between devices, on_device(): tokens_all = lax.all_gather(tokens, both, axis=0, tiled=True)  9.28 us
    convert_element_type x2, other arithmetic, on_device(): whole = whole.astype(BF16)  6.53 us
  transfers between devices with their start and end apart: 7, of which 7 were waited for; matrix products, arithmetic and copies ran while one was open for 15% of the time, Pallas kernels for 0%

profile of v1, /device:TPU:0, one launch (start us, length us, event | category | flops | bytes accessed | tf_op | source)
XLA Modules:
  0.0 253.1 jit_solution(17071755382334042025)
XLA Ops:
  11.3 14.5 %all-gather.1 = f32[8,4,128]{2,1,0:T(4,128)S(1)} all-gather(f32[1,4,128]{2,1,0:T(4,128)S(1)} %maximum_bitcast_fusion), channel_id=2, replica_groups=mesh['groups'=2,'expert'=4,'dp'=2,'inner'=2] {'expert','inner'}, dimensions={0}, use_global_device_ids=true | all-gather | bytes 18432 | tf_op jit(solution)/shard_map/all_gather | solution.py:67
  30.7 1.5 select_reduce_fusion.1
  32.2 9.3 %all-gather.6.cloned.1.call-done = bf16[1024,1024]{1,0:T(8,128)(2,1)} async-done(((bf16[128,1024]{1,0:T(8,128)(2,1)}), bf16[1024,1024]{1,0:T(8,128)(2,1)}) %all-gather.6.cloned.1.call-update) | async-done | bytes 2097168 | tf_op jit(solution)/shard_map/all_gather | solution.py:69
  41.5 4.5 %convolution_convert_fusion = bf16[1152,1024]{1,0:T(8,128)(2,1)S(1)} fusion(pred[1152,1024]{1,0:T(32,128)(4,1)S(1)} %bitcast_compare_fusion, bf16[1024,1024]{1,0:T(8,128)(2,1)} %all-gather.6.cloned.1.call-done), kind=kOutput, calls=%fused_computation.5 | convolution fusion | flops 2417098752 | bytes 5636096 | tf_op jit(solution)/shard_map/dot_general | solution.py:38
  48.0 23.7 %all-gather.8.cloned.1.call-done = bf16[1024,1024]{1,0:T(8,128)(2,1)} async-done(((bf16[128,1024]{1,0:T(8,128)(2,1)}), bf16[1024,1024]{1,0:T(8,128)(2,1)}) %all-gather.8.cloned.1.call-update) | async-done | bytes 2097168 | tf_op jit(solution)/shard_map/all_gather | solution.py:70
  71.7 4.5 %fusion = bf16[1152,1024]{1,0:T(8,128)(2,1)S(1)} fusion(pred[1152,1024]{1,0:T(32,128)(4,1)S(1)} %bitcast_compare_fusion, bf16[1024,1024]{1,0:T(8,128)(2,1)} %all-gather.8.cloned.1.call-done, f32[1152]{0:T(1024)S(1)} %mul.107), kind=kOutput, calls=%fused_computation.6 | convolution fusion | flops 2418278400 | bytes 5640704 | tf_op jit(solution)/shard_map/dot_general | solution.py:38
  79.2 26.6 %collective-permute-done.2 = bf16[384,1536]{1,0:T(8,128)(2,1)S(1)} collective-permute-done((bf16[384,1536]{1,0:T(8,128)(2,1)S(1)}, bf16[384,1536]{1,0:T(8,128)(2,1)S(1)}, u32[]{:S(2)}, u32[]{:S(2)}) %collective-permute-start.2) | collective-permute-done | bytes 1179680 | tf_op jit(solution)/shard_map/ppermute | solution.py:104
  108.2 2.2 convolution_convert_fusion.10
  110.5 1.8 convolution_convert_fusion.11
  113.1 1.5 collective-permute-start.1
  114.6 1.8 convolution_convert_fusion.13
  124.3 17.7 %collective-permute-done.1 = bf16[384,1536]{1,0:T(8,128)(2,1)S(1)} collective-permute-done((bf16[384,1536]{1,0:T(8,128)(2,1)S(1)}, bf16[384,1536]{1,0:T(8,128)(2,1)S(1)}, u32[]{:S(2)}, u32[]{:S(2)}) %collective-permute-start.1) | collective-permute-done | bytes 1179680 | tf_op jit(solution)/shard_map/ppermute | solution.py:104
  142.3 1.5 add_multiply_fusion.1
  143.9 21.8 %collective-permute-done = bf16[384,1536]{1,0:T(8,128)(2,1)S(1)} collective-permute-done((bf16[384,1536]{1,0:T(8,128)(2,1)S(1)}, bf16[384,1536]{1,0:T(8,128)(2,1)S(1)}, u32[]{:S(2)}, u32[]{:S(2)}) %collective-permute-start) | collective-permute-done | bytes 1179680 | tf_op jit(solution)/shard_map/ppermute | solution.py:104
  168.1 1.5 add_convert_fusion
  169.6 27.3 %all-gather.10.cloned.1.call-done = bf16[4,384,1536]{2,1,0:T(8,128)(2,1)} async-done(((bf16[1,384,1536]{2,1,0:T(8,128)(2,1)}), bf16[4,384,1536]{2,1,0:T(8,128)(2,1)}) %all-gather.10.cloned.1.call-update) | async-done | bytes 4718608 | tf_op jit(solution)/shard_map/all_gather | solution.py:123
  196.9 4.3 %fusion.12 = (bf16[384,1536]{1,0:T(8,128)(2,1)}, bf16[384,1536]{1,0:T(8,128)(2,1)S(1)}) fusion(pred[]{:T(512)} %bitcast.38, pred[]{:T(512)} %bitcast.36, pred[]{:T(512)} %bitcast.34, pred[]{:T(512)} %bitcast.32, bf16[4,384,1536]{2,1,0:T(8,128)(2,1)} %all-gather.10.cloned.1.call-done, bf16[384,512]{1,0:T(8,128)(2,1)S(1)} %copy-done.7, ...), kind=kLoop, calls=%fused_computation.26 | loop fusion | flops 12386304 | bytes 8257924 | tf_op jit(solution)/shard_map/convert_element_type | solution.py:144
  203.5 2.2 fusion.6
  207.8 4.2 %fusion.29 = bf16[1024,1024]{1,0:T(8,128)(2,1)} fusion(pred[1152,1024]{1,0:T(32,128)(4,1)S(1)} %copy-done.12, bf16[384,1024]{1,0:T(8,128)(2,1)S(1)} %copy-done.15, bf16[384,1024]{1,0:T(8,128)(2,1)S(1)} %add_convert_fusion.1, bf16[384,1024]{1,0:T(8,128)(2,1)S(1)} %add_convert_fusion.2), kind=kOutput, calls=%fused_computation.53 | convolution fusion | flops 2424045568 | bytes 5636096 | tf_op jit(solution)/shard_map/dot_general | solution.py:38
  213.2 2.0 fusion.33
  216.0 1.5 pad_maximum_fusion
  219.0 1.5 pad_maximum_fusion.1
  222.9 1.5 pad_maximum_fusion.2
  224.4 22.1 %reduce-scatter.2.cloned.1.call-done = bf16[128,1024]{1,0:T(8,128)(2,1)} async-done(((bf16[1024,1024]{1,0:T(8,128)(2,1)}), bf16[128,1024]{1,0:T(8,128)(2,1)}) %reduce-scatter.2.cloned.1.call-update) | async-done | bytes 262160 | tf_op jit(solution)/shard_map/reduce_scatter | solution.py:136
  (115 shorter events, 32.7 us)
Async XLA Ops:
  7.2 40.3 %copy-start = (bf16[1,1024,512]{2,1,0:T(8,128)(2,1)S(1)}, bf16[1,1024,512]{2,1,0:T(8,128)(2,1)}, u32[]{:S(2)}) copy-start(bf16[1,1024,512]{2,1,0:T(8,128)(2,1)} %param.19) | copy-start | bytes 3145732
  7.2 34.3 %all-gather.6.cloned.1.call-start = ((), (), s32[]{:S(2)}) async-start(), calls=%async_computation.1 | async-start | bytes 2359296 | tf_op jit(solution)/shard_map/all_gather | solution.py:69
  7.9 63.8 %all-gather.8.cloned.1.call-start = ((), (), s32[]{:S(2)}) async-start(), calls=%async_computation.2 | async-start | bytes 2359296 | tf_op jit(solution)/shard_map/all_gather | solution.py:70
  8.7 188.2 %all-gather.10.cloned.1.call-start = ((), (), s32[]{:S(2)}) async-start(), calls=%async_computation.4 | async-start | bytes 5898240 | tf_op jit(solution)/shard_map/all_gather | solution.py:123
  30.7 41.0 %copy-start.11 = (pred[1152,1024]{1,0:T(32,128)(4,1)}, pred[1152,1024]{1,0:T(32,128)(4,1)S(1)}, u32[]{:S(2)}) copy-start(pred[1152,1024]{1,0:T(32,128)(4,1)S(1)} %bitcast_compare_fusion) | copy-start | bytes 3538948
  41.5 4.5 %copy-start.13 = (bf16[1,1024,512]{2,1,0:T(8,128)(2,1)S(1)}, bf16[1,1024,512]{2,1,0:T(8,128)(2,1)}, u32[]{:S(2)}) copy-start(bf16[1,1024,512]{2,1,0:T(8,128)(2,1)} %param.20) | copy-start | bytes 3145732
  71.7 4.5 %copy-start.18 = (bf16[1,512,1024]{2,1,0:T(8,128)(2,1)S(1)}, bf16[1,512,1024]{2,1,0:T(8,128)(2,1)}, u32[]{:S(2)}) copy-start(bf16[1,512,1024]{2,1,0:T(8,128)(2,1)} %param.21) | copy-start | bytes 3145732
  77.7 28.1 %collective-permute-start.2 = (bf16[384,1536]{1,0:T(8,128)(2,1)S(1)}, bf16[384,1536]{1,0:T(8,128)(2,1)S(1)}, u32[]{:S(2)}, u32[]{:S(2)}) collective-permute-start(bf16[384,1536]{1,0:T(8,128)(2,1)S(1)} %pad_maximum_fusion.5), channel_id=1, source_target_pairs={{0,2},{2,0},{1,3},{3,1},{4,6},{6,4},{5,7},{7,5},{8,10},{10,8},{9,1... | collective-permute-start | bytes 3538952 | tf_op jit(solution)/shard_map/ppermute | solution.py:104
  108.0 138.6 %reduce-scatter.2.cloned.1.call-start = ((), (), s32[]{:S(2)}) async-start(), calls=%async_computation.3 | async-start | bytes 2359296 | tf_op jit(solution)/shard_map/reduce_scatter | solution.py:136
  108.2 2.2 copy-start.4
  108.2 4.1 %copy-start.22 = (bf16[1152,1024]{1,0:T(8,128)(2,1)S(1)}, bf16[1152,1024]{1,0:T(8,128)(2,1)}, u32[]{:S(2)}) copy-start(bf16[1152,1024]{1,0:T(8,128)(2,1)} %copy-done.21) | copy-start | bytes 7077892
  112.4 2.2 copy-start.17
  113.1 28.9 %collective-permute-start.1 = (bf16[384,1536]{1,0:T(8,128)(2,1)S(1)}, bf16[384,1536]{1,0:T(8,128)(2,1)S(1)}, u32[]{:S(2)}, u32[]{:S(2)}) collective-permute-start(bf16[384,1536]{1,0:T(8,128)(2,1)S(1)} %pad_maximum_fusion.4), channel_id=1, source_target_pairs={{0,2},{2,0},{1,3},{3,1},{4,6},{6,4},{5,7},{7,5},{8,10},{10,8},{9,1... | collective-permute-start | bytes 3538952 | tf_op jit(solution)/shard_map/ppermute | solution.py:104
  117.7 47.9 %collective-permute-start = (bf16[384,1536]{1,0:T(8,128)(2,1)S(1)}, bf16[384,1536]{1,0:T(8,128)(2,1)S(1)}, u32[]{:S(2)}, u32[]{:S(2)}) collective-permute-start(bf16[384,1536]{1,0:T(8,128)(2,1)S(1)} %pad_maximum_fusion.3), channel_id=1, source_target_pairs={{0,2},{2,0},{1,3},{3,1},{4,6},{6,4},{5,7},{7,5},{8,10},{10,8},{9,1... | collective-permute-start | bytes 3538952 | tf_op jit(solution)/shard_map/ppermute | solution.py:104
  168.1 28.9 %copy-start.6 = (bf16[384,512]{1,0:T(8,128)(2,1)S(1)}, bf16[384,512]{1,0:T(8,128)(2,1)}, u32[]{:S(2)}) copy-start(bf16[384,512]{1,0:T(8,128)(2,1)} %get-tuple-element.20) | copy-start | bytes 1179652
  168.1 28.9 %copy-start.7 = (bf16[384,512]{1,0:T(8,128)(2,1)S(1)}, bf16[384,512]{1,0:T(8,128)(2,1)}, u32[]{:S(2)}) copy-start(bf16[384,512]{1,0:T(8,128)(2,1)} %get-tuple-element.21) | copy-start | bytes 1179652
  168.1 28.9 %copy-start.8 = (bf16[384,512]{1,0:T(8,128)(2,1)S(1)}, bf16[384,512]{1,0:T(8,128)(2,1)}, u32[]{:S(2)}) copy-start(bf16[384,512]{1,0:T(8,128)(2,1)} %get-tuple-element.22) | copy-start | bytes 1179652
  196.9 6.6 %slice-start = ((s8[4718592]{0:T(1024)(128)(4,1)}), s8[4194304]{0:T(1024)(128)(4,1)S(1)}, s32[]{:S(2)}) async-start(s8[4718592]{0:T(1024)(128)(4,1)} %bitcast.135), calls=%async_computation.5 | async-start | bytes 8388608
  196.9 4.3 %copy-start.3 = (bf16[2,1024,512]{2,1,0:T(8,128)(2,1)S(1)}, bf16[2,1024,512]{2,1,0:T(8,128)(2,1)}, u32[]{:S(2)}) copy-start(bf16[2,1024,512]{2,1,0:T(8,128)(2,1)} %param.16) | copy-start | bytes 6291460
  196.9 6.5 %slice-start.1 = ((s8[4718592]{0:T(1024)(128)(4,1)}), s8[524288]{0:T(1024)(128)(4,1)S(1)}, s32[]{:S(2)}) async-start(s8[4718592]{0:T(1024)(128)(4,1)} %bitcast.135), calls=%async_computation.6 | async-start | bytes 1048576
  212.0 3.3 %copy-start.10 = (bf16[384,1536]{1,0:T(8,128)(2,1)S(1)}, bf16[384,1536]{1,0:T(8,128)(2,1)}, u32[]{:S(2)}) copy-start(bf16[384,1536]{1,0:T(8,128)(2,1)} %get-tuple-element.13) | copy-start | bytes 3538948
  212.0 3.3 %copy-start.23 = (bf16[1152,1024]{1,0:T(8,128)(2,1)S(1)}, bf16[1152,1024]{1,0:T(8,128)(2,1)}, u32[]{:S(2)}) copy-start(bf16[1152,1024]{1,0:T(8,128)(2,1)} %copy-done.21) | copy-start | bytes 7077892
  219.0 2.4 copy-start.20
  222.2 24.4 %copy-start.1 = (bf16[1,1024,512]{2,1,0:T(8,128)(2,1)S(1)}, bf16[1,1024,512]{2,1,0:T(8,128)(2,1)}, u32[]{:S(2)}) copy-start(bf16[1,1024,512]{2,1,0:T(8,128)(2,1)} %param.19) | copy-start | bytes 3145732
  (9 other events, 13.3 us)
Sparse Core Ops, SparseCore 0:
  9.6 31.8 all-gather.5
  43.1 28.5 all-gather.7
  108.1 88.7 all-gather.9
  212.1 34.4 reduce-scatter.1
